TPU v7x, 1024 devices: a whole 4x8x16 slice. The times are simulated.
1024 devices in a mesh: orb: 64 (over y, x, core), grid: 16 (over z).
Axes of the slice: x: 4, y: 8, z: 16, core: 2. Of those that a mesh axis runs over, the one named last changes fastest.
Arguments:
- wavefunctions: float32 [512, 96, 1024], P('orb', 'grid'), may hold values from -2 to 2
- potential: float32 [96, 1024], P('grid'), may hold values from -3 to 0
Outputs:
- orbitals: float32 [512, 96, 1024], P('orb', 'grid')
All inputs are finite; a program needn't handle non-finite values.
Results may differ from a plain program's by a relative error of at most 0.0003.
Values sent between devices are 32-bit elements; how exact they have to be, the bound alone decides.
A program may use at most 32 MiB of HBM per device.

v0:
```python
import jax
import jax.numpy as jnp
from jax import lax
from jax.sharding import PartitionSpec as P

PANEL = 32
NPANEL = 2
NY = 32


COEFFS = (
    -5369.0 / 1800.0,
    12.0 / 7.0,
    -15.0 / 56.0,
    10.0 / 189.0,
    -1.0 / 112.0,
    2.0 / 1925.0,
    -1.0 / 16632.0,
)
HIGH = lax.Precision.HIGHEST
RIM = 6


def from_root(shard, axis, root):
    mine = lax.axis_index(axis) == root
    return lax.psum(jnp.where(mine, shard, jnp.zeros_like(shard)), axis)


def extended_2(shard, sides, width):
    for axis, dim in sides:
        peers, length = (lax.axis_size(axis), shard.shape[dim])
        up = [(i, (i + 1) % peers) for i in range(peers)]
        down = [(j, i) for i, j in up]
        last = lax.slice_in_dim(shard, length - width, length, axis=dim)
        first = lax.slice_in_dim(shard, 0, width, axis=dim)
        before = lax.ppermute(last, axis, up)
        after = lax.ppermute(first, axis, down)
        shard = jnp.concatenate([before, shard, after], axis=dim)
    return shard


def inner(left, right, scale):
    return jnp.einsum("ic,jc->ij", left, right, precision=HIGH) * scale


def orthonormalize(block, gram):
    lower = jnp.linalg.cholesky(gram)
    return lax.linalg.triangular_solve(lower, block, left_side=True, lower=True)


def fetch_panel(work, first, members):
    pieces = []
    for member in range(members):
        pieces.append(from_root(work, "orb", first + member))
    return jnp.concatenate(pieces, 0)


def panel_gram_sum(block, scale):
    return lax.psum(inner(block, block, scale), "grid")


def coefficient_sum(local):
    return lax.psum(local, "grid")


def remove(block, coeff, ortho):
    return block - jnp.einsum("ij,ic->jc", coeff, ortho, precision=HIGH)


def update(work, moved, ortho, rank, first, members):
    count = work.shape[0]
    offset = jnp.clip(rank - first, 0, members - 1) * count
    owned = lax.dynamic_slice_in_dim(ortho, offset, count, 0)
    member = (rank >= first) & (rank < first + members)
    later = rank >= first + members
    return jnp.where(later, moved, jnp.where(member, owned, work))


def per_device(wavefunctions, potential):
    count, depth, plane = wavefunctions.shape
    cells = depth * plane
    members = PANEL // count
    scale = 1.0 / (depth * plane * lax.axis_size("grid"))
    extended = extended_2(wavefunctions, (("grid", 1),), RIM)
    margin = RIM * NY
    padded = jnp.pad(wavefunctions, ((0, 0), (0, 0), (margin, margin)))
    column = lax.broadcasted_iota(jnp.int32, (plane,), 0) % NY
    total = 3.0 * COEFFS[0] * wavefunctions
    for k in range(1, RIM + 1):
        along_z = extended[:, RIM + k : RIM + k + depth] + extended[:, RIM - k : RIM - k + depth]
        along_x = (
            padded[:, :, margin + k * NY : margin + k * NY + plane]
            + padded[:, :, margin - k * NY : margin - k * NY + plane]
        )
        y_plus = jnp.where(column + k < NY, padded[:, :, margin + k : margin + k + plane], 0.0)
        y_minus = jnp.where(column - k >= 0, padded[:, :, margin - k : margin - k + plane], 0.0)
        total = total + COEFFS[k] * (along_z + along_x + y_plus + y_minus)
    work = -0.5 * total.reshape(count, cells) + (potential[None] * wavefunctions).reshape(
        count, cells
    )
    rank = lax.axis_index("orb")
    panel = fetch_panel(work, 0, members)
    for p in range(NPANEL):
        gram = panel_gram_sum(panel, scale)
        ortho = orthonormalize(panel, gram)
        coeff = coefficient_sum(inner(ortho, work, scale))
        work = update(work, remove(work, coeff, ortho), ortho, rank, p * members, members)
        if p + 1 < NPANEL:
            panel = fetch_panel(work, (p + 1) * members, members)
    return work.reshape(count, depth, plane)


def solution(mesh):
    return jax.shard_map(
        per_device,
        mesh=mesh,
        in_specs=(P("orb", "grid", None), P("grid", None)),
        out_specs=P("orb", "grid", None),
        check_vma=False,
    )
```

profile of v0, /device:TPU:2, one launch (start us, length us, event | category | flops | bytes accessed | tf_op | source)
XLA Modules:
  0.0 717.8 jit_solution(14313548568039217298)
XLA Ops:
  6.5 0.0 all-reduce.8.cloned.1.call-start
  6.5 4.3 collective-permute-start.1
  10.8 15.9 %collective-permute-start = (f32[8,6,1024]{2,0,1:T(8,128)}, f32[8,6,1024]{2,0,1:T(8,128)S(1)}, u32[]{:S(2)}, u32[]{:S(2)}) collective-permute-start(f32[8,6,1024]{2,0,1:T(8,128)} %param.5), channel_id=1, source_target_pairs={{1,0},{2,1},{3,2},{4,3},{5,4},{6,5},{7,6},{8,7},{9,8},{10,9},{11,1... | collective-permute-start | bytes 589832 | tf_op jit(solution)/shard_map/ppermute | solution.py:37
  26.8 0.0 copy-start
  26.8 3.1 collective-permute-done.1
  29.9 0.0 copy-done
  29.9 1.2 collective-permute-done
  31.1 0.0 copy-start.7
  31.2 0.7 copy-done.7
  31.9 1.2 fusion.14
  33.1 0.9 broadcast_select_fusion.4
  33.9 0.0 all-reduce.8.cloned.1.call-update
  34.0 0.0 all-reduce.6.cloned.1.call-start
  34.0 214.7 %all-reduce.8.cloned.1.call-done = (f32[8,6144]{1,0:T(8,128)}, f32[8,6144]{1,0:T(8,128)}, f32[8,6144]{1,0:T(8,128)}, f32[8,6144]{1,0:T(8,128)}) async-done(((f32[8,6144]{1,0:T(8,128)}, f32[8,6144]{1,0:T(8,128)}, f32[8,6144]{1,0:T(8,128)}, f32[8,6144]{1,0:T(8,128)}), (f32[8,6144]{1,0:T(8,128)}, f32[8,6144]{1,0:T(8,128)}, f32[8,6144]{1,0:T(8,128)}, f32[8,6144]{1,0:T(8,128)})) %all-reduce.8.cloned.1.call-update) | async-done | bytes 786448 | tf_op jit(solution)/shard_map/psum | solution.py:26
  248.8 0.0 copy-start.4
  248.8 1.0 constant_dynamic-update-slice_fusion.7
  249.7 0.0 copy-done.4
  249.8 0.0 copy-start.2
  249.8 0.9 copy-done.2
  250.7 0.9 copy-done.1
  251.6 0.8 convolution_multiply_fusion.1
  252.4 57.9 %psum.88 = f32[32,32]{0,1:T(8,128)S(1)} all-reduce(f32[32,32]{0,1:T(8,128)S(1)} %convolution_multiply_fusion.1), channel_id=1, replica_groups=mesh['orb'=64,'grid'=16] {'grid'}, use_global_device_ids=true, to_apply=%region_4.5 | all-reduce | flops 1024 | bytes 8192 | tf_op jit(solution)/shard_map/psum | solution.py:59
  310.4 0.1 copy.4
  310.4 2.9 cholesky.44
  313.4 0.6 compare_reduce_fusion.1
  314.0 0.7 fusion.52
  314.7 2.4 custom-call.6
  317.1 0.8 fusion.57
  318.0 0.8 convolution_multiply_fusion.3
  318.7 53.0 %psum.89 = f32[32,8]{1,0:T(8,128)S(1)} all-reduce(f32[32,8]{1,0:T(8,128)S(1)} %convolution_multiply_fusion.3), channel_id=1, replica_groups=mesh['orb'=64,'grid'=16] {'grid'}, use_global_device_ids=true, to_apply=%region_7.10 | all-reduce | flops 256 | bytes 2048 | tf_op jit(solution)/shard_map/psum | solution.py:63
  371.7 1.4 broadcast_select_fusion
  373.1 0.0 all-reduce.6.cloned.1.call-update
  373.2 213.6 %all-reduce.6.cloned.1.call-done = (f32[8,6144]{1,0:T(8,128)}, f32[8,6144]{1,0:T(8,128)}, f32[8,6144]{1,0:T(8,128)}, f32[8,6144]{1,0:T(8,128)}) async-done(((f32[8,6144]{1,0:T(8,128)}, f32[8,6144]{1,0:T(8,128)}, f32[8,6144]{1,0:T(8,128)}, f32[8,6144]{1,0:T(8,128)}), (f32[8,6144]{1,0:T(8,128)}, f32[8,6144]{1,0:T(8,128)}, f32[8,6144]{1,0:T(8,128)}, f32[8,6144]{1,0:T(8,128)})) %all-reduce.6.cloned.1.call-update) | async-done | bytes 786448 | tf_op jit(solution)/shard_map/psum | solution.py:26
  586.8 1.0 constant_dynamic-update-slice_fusion.11
  587.8 0.0 copy-done.6
  587.8 0.9 copy-done.5
  588.8 0.9 copy-done.3
  589.7 0.8 convolution_multiply_fusion
  590.5 57.9 %psum.94 = f32[32,32]{0,1:T(8,128)S(1)} all-reduce(f32[32,32]{0,1:T(8,128)S(1)} %convolution_multiply_fusion), channel_id=1, replica_groups=mesh['orb'=64,'grid'=16] {'grid'}, use_global_device_ids=true, to_apply=%region_12.15 | all-reduce | flops 1024 | bytes 8192 | tf_op jit(solution)/shard_map/psum | solution.py:59
  648.4 0.1 copy.6
  648.5 2.9 cholesky.55
  651.4 0.6 compare_reduce_fusion
  652.1 0.7 fusion.53
  652.7 2.4 custom-call.7
  655.2 0.8 fusion.54
  656.0 0.8 convolution_multiply_fusion.2
  656.8 53.0 %psum.95 = f32[32,8]{1,0:T(8,128)S(1)} all-reduce(f32[32,8]{1,0:T(8,128)S(1)} %convolution_multiply_fusion.2), channel_id=1, replica_groups=mesh['orb'=64,'grid'=16] {'grid'}, use_global_device_ids=true, to_apply=%region_13.16 | all-reduce | flops 256 | bytes 2048 | tf_op jit(solution)/shard_map/psum | solution.py:63
  709.8 1.2 fusion.1
  (23 shorter events, 0.3 us)
Async XLA Ops:
  6.5 242.2 %all-reduce.8.cloned.1.call-start = ((), (), s32[]{:S(2)}) async-start(), calls=%async_computation.1 | async-start | bytes 1572864 | tf_op jit(solution)/shard_map/psum | solution.py:26
  6.5 23.3 %collective-permute-start.1 = (f32[8,6,1024]{2,0,1:T(8,128)}, f32[8,6,1024]{2,0,1:T(8,128)S(1)}, u32[]{:S(2)}, u32[]{:S(2)}) collective-permute-start(f32[8,6,1024]{2,0,1:T(8,128)} %param.5), channel_id=1, source_target_pairs={{0,1},{1,2},{2,3},{3,4},{4,5},{5,6},{6,7},{7,8},{8,9},{9,10},{10,1... | collective-permute-start | bytes 589832 | tf_op jit(solution)/shard_map/ppermute | solution.py:36
  10.8 20.3 %collective-permute-start = (f32[8,6,1024]{2,0,1:T(8,128)}, f32[8,6,1024]{2,0,1:T(8,128)S(1)}, u32[]{:S(2)}, u32[]{:S(2)}) collective-permute-start(f32[8,6,1024]{2,0,1:T(8,128)} %param.5), channel_id=1, source_target_pairs={{1,0},{2,1},{3,2},{4,3},{5,4},{6,5},{7,6},{8,7},{9,8},{10,9},{11,1... | collective-permute-start | bytes 589832 | tf_op jit(solution)/shard_map/ppermute | solution.py:37
  26.8 3.1 copy-start
  31.1 0.8 copy-start.7
  34.0 552.8 %all-reduce.6.cloned.1.call-start = ((), (), s32[]{:S(2)}) async-start(), calls=%async_computation | async-start | bytes 1572864 | tf_op jit(solution)/shard_map/psum | solution.py:26
  248.8 1.0 copy-start.4
  249.8 0.9 copy-start.2
  250.7 0.9 copy-start.1
  586.8 1.0 copy-start.6
  587.8 0.9 copy-start.5
  588.8 0.9 copy-start.3
Sparse Core Ops, SparseCore 0:
  34.1 214.6 all-reduce.7
  373.3 213.4 all-reduce.5
where the time goes:
time: 718 us
  waiting for transfers between devices  433 us (60%)
  blocking collectives  222 us (31%)
  starting transfers between devices  20.2 us (3%)
  other arithmetic  15.5 us (2%)
  between operations  13.6 us (2%)
  matrix products  7.28 us (1%)
    psum x2, waiting for transfers between devices, from_root(): return lax.psum(jnp.where(mine, shard, jnp.zeros_like(shard)), axis)  428 us
    psum x2, blocking collectives, panel_gram_sum(): return lax.psum(inner(block, block, scale), 'grid')  116 us
    psum x2, blocking collectives, coefficient_sum(): return lax.psum(local, 'grid')  106 us
    ppermute x1, starting transfers between devices, extended_2(): after = lax.ppermute(first, axis, down)  15.9 us
  transfers between devices with their start and end apart: 4, of which 4 were waited for; matrix products, arithmetic and copies ran while one was open for 0% of the time, Pallas kernels for 0%

commit v1 on v0

v1 whole, which is shorter than its diff:
```python
import functools

import jax
import jax.numpy as jnp
from jax import lax
from jax.experimental import pallas as pl
from jax.experimental.pallas import tpu as pltpu
from jax.sharding import PartitionSpec as P

PANEL = 32
NPANEL = 2
NY = 32
NXC = 4
ROWS = PANEL * NPANEL

COEFFS = (
    -5369.0 / 1800.0,
    12.0 / 7.0,
    -15.0 / 56.0,
    10.0 / 189.0,
    -1.0 / 112.0,
    2.0 / 1925.0,
    -1.0 / 16632.0,
)
RIM = 6
MESH = pl.DeviceIdType.MESH
F32 = jnp.float32
BF16 = jnp.bfloat16


def split(value):
    high = value.astype(BF16)
    return high, (value - high.astype(F32)).astype(BF16)


def nt(left, right):
    return lax.dot_general(left, right, (((1,), (1,)), ((), ())), preferred_element_type=F32)


def in_plane(v, v0_term):
    width = v.shape[1]
    lane = lax.broadcasted_iota(jnp.int32, v.shape, 1)
    column = lane % NY
    total = v0_term
    for k in range(1, RIM + 1):
        far = k * NY
        part = jnp.where(lane < width - far, pltpu.roll(v, width - far, 1), 0.0)
        part += jnp.where(lane >= far, pltpu.roll(v, far, 1), 0.0)
        part += jnp.where(column < NY - k, pltpu.roll(v, width - k, 1), 0.0)
        part += jnp.where(column >= k, pltpu.roll(v, k, 1), 0.0)
        total += (-0.5 * COEFFS[k]) * part
    return total


def order_of(depth):
    return sorted(range(depth), key=lambda p: (max(depth - p, p + 1), p))


def gather_kernel(
    scale, v_ref, pot_ref, work_ref, pieces_ref, gram_ref, coef_ref,
    own, halo, panel, part, zbuf, rest,
    hsend, hrecv, asend, arecv, zsend, zrecv, gsend, grecv,
):
    count, depth, plane = v_ref.shape
    nz, norb = lax.axis_size("grid"), lax.axis_size("orb")
    ny = norb // (2 * NXC)
    z, o = lax.axis_index("grid"), lax.axis_index("orb")
    y, x, c = o // (2 * NXC), (o // 2) % NXC, o % 2

    def at(yy, xx, cc):
        return (yy * NXC + xx) * 2 + cc

    partner = at(y, x, 1 - c)
    right, left = at(y, (x + 1) % NXC, c), at(y, (x + NXC - 1) % NXC, c)
    y_up, y_down = at((y + 1) % ny, x, c), at((y + ny - 1) % ny, x, c)
    order = order_of(depth)

    barrier = pltpu.get_barrier_semaphore()

    def greet_z(d, carry):
        pl.semaphore_signal(barrier, inc=1, device_id=(o, (z + d) % nz), device_id_type=MESH)
        return carry

    def greet_y(d, carry):
        pl.semaphore_signal(barrier, inc=1, device_id=(at((y + d) % ny, x, c), z), device_id_type=MESH)
        return carry

    lax.fori_loop(1, nz, greet_z, 0)
    lax.fori_loop(1, ny, greet_y, 0)
    for peer in (partner, right, left):
        pl.semaphore_signal(barrier, inc=1, device_id=(peer, z), device_id_type=MESH)

    for p in range(depth):
        own[p] = v_ref[:, p, :]

    pl.semaphore_wait(barrier, (nz - 1) + (ny - 1) + 3)

    halo_copies = []
    for i in range(depth):
        for side, p, peer in ((0, depth - 1 - i, (z + 1) % nz), (1, i, (z + nz - 1) % nz)):
            copy = pltpu.make_async_remote_copy(
                src_ref=own.at[p],
                dst_ref=halo.at[side, p],
                send_sem=hsend.at[side, p],
                recv_sem=hrecv.at[side, p],
                device_id=(o, peer),
                device_id_type=MESH,
            )
            copy.start()
            halo_copies.append(copy)
    arrived = {(0, depth - 1 - i // 2) if i % 2 == 0 else (1, i // 2): copy for i, copy in enumerate(halo_copies)}

    def flat(p, carry):
        v = own[p]
        rest[p] = in_plane(v, (pot_ref[pl.ds(p, 1), :] - 1.5 * COEFFS[0]) * v)
        return carry

    lax.fori_loop(0, depth, flat, 0)

    def slab(xx, cc):
        return (xx % NXC) * 2 + cc

    mine = slab(x, c)

    def copy_of(kind, s, p, peer):
        rows = pl.ds(pl.multiple_of(s * count, count), count)
        return pltpu.make_async_remote_copy(
            src_ref=panel.at[p, rows, :],
            dst_ref=panel.at[p, rows, :],
            send_sem=asend.at[kind, p],
            recv_sem=arecv.at[s, p],
            device_id=(peer, z),
            device_id_type=MESH,
        )

    goes_up = y <= ny // 2 - 1
    goes_down = (y == 0) | (y >= ny // 2 + 2)

    seen = set()
    for p in order:
        need = [(0, q) for q in range(p, depth)] + [(1, q) for q in range(0, p + 1)]
        for key in need:
            if key not in seen:
                seen.add(key)
                arrived[key].wait_recv()
        total = rest[p]
        for k in range(1, RIM + 1):
            after = own[p + k] if p + k < depth else halo[1, p + k - depth]
            before = own[p - k] if p - k >= 0 else halo[0, p - k + depth]
            total += (-0.5 * COEFFS[k]) * (after + before)
        work_ref[p] = total

        @pl.when(y == 0)
        def _():
            panel[p, pl.ds(pl.multiple_of(mine * count, count), count), :] = total
            copy_of(0, mine, p, y_up).start()
            copy_of(1, mine, p, y_down).start()
            copy_of(2, mine, p, right).start()
            copy_of(3, mine, p, left).start()
            copy_of(5, mine, p, partner).start()

    lag_near, lag_far = 2, 4
    half = depth // 2
    for t in range(depth + lag_far):
        if t < depth:
            p = order[t]

            @pl.when(y != 0)
            def _():
                copy_of(0, mine, p, y_up).wait_recv()
                copy_of(2, mine, p, right).start()
                copy_of(3, mine, p, left).start()
                copy_of(5, mine, p, partner).start()

                @pl.when(goes_up)
                def _():
                    copy_of(0, mine, p, y_up).start()

                @pl.when(goes_down)
                def _():
                    copy_of(1, mine, p, y_down).start()

        i = t - lag_near
        if 0 <= i < depth:
            p = order[i]
            from_left, from_right = slab(x + NXC - 1, c), slab(x + 1, c)
            copy_of(2, from_left, p, right).wait_recv()
            if i % 2 == 0:
                copy_of(4, from_left, p, right).start()
            copy_of(6, from_left, p, partner).start()
            copy_of(3, from_right, p, left).wait_recv()
            if i % 2 == 1:
                copy_of(4, from_right, p, left).start()
            copy_of(7, from_right, p, partner).start()
        i = t - lag_far
        if 0 <= i < depth:
            p = order[i]
            far = slab(x + 2, c)
            copy_of(4, far, p, right).wait_recv()
            copy_of(8, far, p, partner).start()

    part[...] = jnp.zeros_like(part)
    for p in order:
        for xx in range(NXC):
            copy_of(5, slab(xx, 1 - c), p, partner).wait_recv()
        high, low = split(panel[p])
        pieces = jnp.concatenate([high, low], axis=0)
        pieces_ref[p] = pieces

        @pl.when(y == 0)
        def _():
            product = nt(pieces, pieces)
            part[...] += product[:ROWS] + product[ROWS:]

        @pl.when(y != 0)
        def _():
            own_high, own_low = split(work_ref[p])
            product = nt(jnp.concatenate([own_high, own_low], axis=0), pieces)
            part[0:count] += product[:count] + product[count:]

    half_rows = ROWS // 2

    @pl.when(y == 0)
    def _():
        both = part[...]
        both = (both + pltpu.roll(both, ROWS, 1)) * scale
        lane = lax.broadcasted_iota(jnp.int32, (half_rows, 2 * ROWS), 1)
        zbuf[z] = jnp.where(lane < ROWS, both[:half_rows], both[half_rows:])

    @pl.when(y != 0)
    def _():
        both = part[0:count]
        zbuf[z, 0:count] = (both + pltpu.roll(both, ROWS, 1)) * scale

    def z_copy(origin, to, slot, rows):
        return pltpu.make_async_remote_copy(
            src_ref=zbuf.at[origin, pl.ds(0, rows), :],
            dst_ref=zbuf.at[origin, pl.ds(0, rows), :],
            send_sem=zsend.at[slot],
            recv_sem=zrecv.at[origin],
            device_id=(o, to),
            device_id_type=MESH,
        )

    def exchange(rows):
        def send(d, carry):
            z_copy(z, (z + d) % nz, d, rows).start()
            return carry

        def take(d, carry):
            z_copy((z + d) % nz, z, 0, rows).wait_recv()
            return carry

        def sent(d, carry):
            z_copy(z, (z + d) % nz, d, rows).wait_send()
            return carry

        lax.fori_loop(1, nz, send, 0)
        lax.fori_loop(1, nz, take, 0)
        total = zbuf[0, 0:rows]
        for i in range(1, 16):
            total += zbuf[i, 0:rows]
        lax.fori_loop(1, nz, sent, 0)
        return total

    def g_copy(d):
        return pltpu.make_async_remote_copy(
            src_ref=gram_ref,
            dst_ref=gram_ref,
            send_sem=gsend.at[d],
            recv_sem=grecv,
            device_id=(at((y + d) % ny, x, c), z),
            device_id_type=MESH,
        )

    @pl.when(y == 0)
    def _():
        gram_ref[...] = exchange(half_rows)
        coef_ref[...] = jnp.zeros_like(coef_ref)
        for d in range(1, 8):
            g_copy(d).start()
        for d in range(1, 8):
            g_copy(d).wait_send()

    @pl.when(y != 0)
    def _():
        coef_ref[...] = exchange(count)
        g_copy(1).wait_recv()

    for copy in halo_copies:
        copy.wait_send()
    for p in range(depth):

        @pl.when(goes_up)
        def _():
            copy_of(0, mine, p, y_up).wait_send()

        @pl.when(goes_down)
        def _():
            copy_of(1, mine, p, y_down).wait_send()

        for kind in range(2, 9):
            copy_of(kind, mine, p, partner).wait_send()


def correct_kernel(work_ref, pieces_ref, gram_ref, coef_ref, out_ref, inverse):
    count, depth, plane = out_ref.shape
    o = lax.axis_index("orb")
    half_rows = ROWS // 2
    packed = gram_ref[...]
    row = lax.broadcasted_iota(jnp.int32, (ROWS, 2 * ROWS), 0)
    lane = lax.broadcasted_iota(jnp.int32, (ROWS, 2 * ROWS), 1)
    full = jnp.concatenate([packed, pltpu.roll(packed, ROWS, 1)], axis=0)
    matrix = jnp.where(lane < ROWS, full, jnp.where(lane - ROWS == row, 1.0, 0.0))
    for k in range(ROWS - 1):
        base = (k // 8) * 8
        pivot_row = matrix[k : k + 1, :]
        scaled = pivot_row / matrix[k : k + 1, k : k + 1]
        below = matrix[base:, :]
        column = below[:, k : k + 1]
        below_row = row[base:, 0:1]
        column = jnp.where(below_row > k, column, 0.0)
        below = below - column * scaled
        matrix = below if base == 0 else jnp.concatenate([matrix[:base], below], axis=0)
    diagonal = jnp.sum(jnp.where(lane == row, matrix, 0.0), axis=1, keepdims=True)
    inverse[...] = matrix * lax.rsqrt(diagonal)

    lower_inverse = pltpu.roll(inverse[...], ROWS, 1)[:, :ROWS]
    coef = coef_ref[:, :ROWS]
    high = lax.Precision.HIGHEST
    solved = lax.dot_general(coef, lower_inverse, (((1,), (1,)), ((), ())), precision=high, preferred_element_type=F32)
    factor = -lax.dot_general(solved, lower_inverse, (((1,), (0,)), ((), ())), precision=high, preferred_element_type=F32)
    in_panel = o * count < ROWS
    start = pl.multiple_of(jnp.minimum(o * count, ROWS - count), count)
    rows = pltpu.roll(inverse[pl.ds(start, count), :], ROWS, 1)[:, :ROWS]
    factor = jnp.where(in_panel, rows, factor)
    keep = jnp.where(in_panel, 0.0, 1.0)
    f_high, f_low = split(factor)
    both = jnp.concatenate([jnp.concatenate([f_high, f_high], axis=1), jnp.concatenate([f_low, f_low], axis=1)], axis=0)
    for p in range(depth):
        product = jnp.dot(both, pieces_ref[p], preferred_element_type=F32)
        out_ref[:, p, :] = keep * work_ref[p] + (product[:count] + product[count:])


def per_device(wavefunctions, potential):
    count, depth, plane = wavefunctions.shape
    nz, ny = lax.axis_size("grid"), lax.axis_size("orb") // (2 * NXC)
    scale = 1.0 / (depth * plane * nz)
    vmem = pl.BlockSpec(memory_space=pltpu.VMEM)
    dma = pltpu.SemaphoreType.DMA
    work, pieces, gram, coef = pl.pallas_call(
        functools.partial(gather_kernel, scale),
        out_shape=(
            jax.ShapeDtypeStruct((depth, count, plane), F32),
            jax.ShapeDtypeStruct((depth, 2 * ROWS, plane), BF16),
            jax.ShapeDtypeStruct((ROWS // 2, 2 * ROWS), F32),
            jax.ShapeDtypeStruct((count, 2 * ROWS), F32),
        ),
        in_specs=[vmem, vmem],
        out_specs=(vmem, vmem, vmem, vmem),
        scratch_shapes=[
            pltpu.VMEM((depth, count, plane), F32),
            pltpu.VMEM((2, depth, count, plane), F32),
            pltpu.VMEM((depth, ROWS, plane), F32),
            pltpu.VMEM((ROWS, 2 * ROWS), F32),
            pltpu.VMEM((nz, ROWS // 2, 2 * ROWS), F32),
            pltpu.VMEM((depth, count, plane), F32),
            dma((2, depth)),
            dma((2, depth)),
            dma((9, depth)),
            dma((2 * NXC, depth)),
            dma((nz,)),
            dma((nz,)),
            dma((ny,)),
            dma,
        ],
        compiler_params=pltpu.CompilerParams(collective_id=0, has_side_effects=True),
        name="gather",
    )(wavefunctions, potential)
    return pl.pallas_call(
        correct_kernel,
        out_shape=jax.ShapeDtypeStruct((count, depth, plane), F32),
        in_specs=[vmem] * 4,
        out_specs=vmem,
        scratch_shapes=[pltpu.VMEM((ROWS, 2 * ROWS), F32)],
        name="correct",
    )(work, pieces, gram, coef)


def solution(mesh):
    return jax.shard_map(
        per_device,
        mesh=mesh,
        in_specs=(P("orb", "grid", None), P("grid", None)),
        out_specs=P("orb", "grid", None),
        check_vma=False,
    )
```

time: 718 us -> 76.3 us (0.11)
  the two profiles are of different devices: /device:TPU:2 before, /device:TPU:32 now
where the time goes in v1:
time: 76.3 us; the launch traced here: 76.1 us
  Pallas kernels  72.6 us (95%)
  local copies, waits for them, and re-layouts  3.49 us (5%)
    pallas_call x1, Pallas kernels, per_device(): pl.pallas_call(functools.partial(gather_kernel, scale), out_shape=(jax.Sh...  64.3 us
    pallas_call x1, Pallas kernels, per_device(): pl.pallas_call(correct_kernel, out_shape=jax.ShapeDtypeStruct((count, dep...  8.27 us
    unnamed x1, local copies, waits for them, and re-layouts  1.75 us
    pallas_call x1, local copies, waits for them, and re-layouts, per_device(): pl.pallas_call(correct_kernel, out_shape=jax.ShapeDtypeStruct((count, dep...  1.74 us

profile of v1, /device:TPU:32, one launch (start us, length us, event | category | flops | bytes accessed | tf_op | source)
XLA Modules:
  0.0 76.1 jit_solution(14954994797269004551)
XLA Ops:
  0.0 1.8 %copy.3.v_ref = f32[8,6,1024]{2,1,0:T(8,128)} copy(f32[8,6,1024]{2,0,1:T(8,128)} %param.2) | data formatting | bytes 393216 | tf_op args[0]
  1.8 64.3 %gather.1 = (f32[6,8,1024]{2,1,0:T(8,128)}, bf16[6,128,1024]{2,1,0:T(8,128)(2,1)}, f32[32,128]{1,0:T(8,128)}, f32[8,128]{1,0:T(8,128)}) custom-call(f32[8,6,1024]{2,1,0:T(8,128)} %copy.3.v_ref, f32[6,1024]{1,0:T(8,128)} %pot_ref.1), custom_call_target="tpu_custom_call" | custom-call | tf_op jit(solution)/shard_map/gather/pallas_call | solution.py:351
  66.1 8.3 %correct.1 = f32[8,6,1024]{2,1,0:T(8,128)} custom-call(f32[6,8,1024]{2,1,0:T(8,128)} %get-tuple-element.9.work_ref, bf16[6,128,1024]{2,1,0:T(8,128)(2,1)} %get-tuple-element.10.pieces_ref, f32[32,128]{1,0:T(8,128)} %get-tuple-element.11.gram_ref, f32[8,128]{1,0:T(8,128)} %get-tuple-element.12.coef_ref), custom_call_target="tpu_custom_call" | custom-call | tf_op jit(solution)/shard_map/correct/pallas_call | solution.py:380
  74.3 1.7 %copy.4 = f32[8,6,1024]{2,0,1:T(8,128)} copy(f32[8,6,1024]{2,1,0:T(8,128)} %correct.1) | data formatting | bytes 393216 | tf_op jit(solution)/shard_map/correct/pallas_call | solution.py:380

commit v2 on v1

v2 whole, which is shorter than its diff:
```python
import functools

import jax
import jax.numpy as jnp
from jax import lax
from jax.experimental import pallas as pl
from jax.experimental.pallas import tpu as pltpu
from jax.sharding import PartitionSpec as P

PANEL = 32
NPANEL = 2
NY = 32
NXC = 4
ROWS = PANEL * NPANEL

COEFFS = (
    -5369.0 / 1800.0,
    12.0 / 7.0,
    -15.0 / 56.0,
    10.0 / 189.0,
    -1.0 / 112.0,
    2.0 / 1925.0,
    -1.0 / 16632.0,
)
RIM = 6
MESH = pl.DeviceIdType.MESH
LAGS = (3, 6)
F32 = jnp.float32
BF16 = jnp.bfloat16


def split(value):
    high = value.astype(BF16)
    return high, (value - high.astype(F32)).astype(BF16)


def nt(left, right):
    return lax.dot_general(left, right, (((1,), (1,)), ((), ())), preferred_element_type=F32)


def in_plane(v, v0_term):
    width = v.shape[1]
    lane = lax.broadcasted_iota(jnp.int32, v.shape, 1)
    column = lane % NY
    total = v0_term
    for k in range(1, RIM + 1):
        far = k * NY
        part = jnp.where(lane < width - far, pltpu.roll(v, width - far, 1), 0.0)
        part += jnp.where(lane >= far, pltpu.roll(v, far, 1), 0.0)
        part += jnp.where(column < NY - k, pltpu.roll(v, width - k, 1), 0.0)
        part += jnp.where(column >= k, pltpu.roll(v, k, 1), 0.0)
        total += (-0.5 * COEFFS[k]) * part
    return total


def order_of(depth):
    return sorted(range(depth), key=lambda p: (max(depth - p, p + 1), p))


def eliminate(packed):
    row = lax.broadcasted_iota(jnp.int32, (8, 2 * ROWS), 0)
    lane = lax.broadcasted_iota(jnp.int32, (8, 2 * ROWS), 1)
    rolled = pltpu.roll(packed, ROWS, 1)
    tiles, pivots = [], []
    for t in range(ROWS // 8):
        source = rolled if t < ROWS // 16 else packed
        r = (t * 8) % (ROWS // 2)
        tiles.append(jnp.where(lane >= ROWS, source[r : r + 8], jnp.where(lane == row + t * 8, 1.0, 0.0)))
        pivots.append(jnp.ones((8, 2 * ROWS), F32))

    def spread(tile, r):
        return jnp.broadcast_to(tile[r : r + 1, :], tile.shape)

    width = 4
    for k in range(0, ROWS, width):
        b, r = k // 8, k % 8
        below = range(b, ROWS // 8)
        columns = [
            {t: jnp.broadcast_to(tiles[t][:, ROWS + k + j : ROWS + k + j + 1], (8, 2 * ROWS)) for t in below}
            for j in range(width)
        ]
        rows = [spread(tiles[b], r + i) for i in range(width)]
        square = [[spread(columns[j][b], r + i) for j in range(width)] for i in range(width)]
        for i in range(width):
            inverse = 1.0 / square[i][i]
            pivots[b] = jnp.where(row == r + i, square[i][i], pivots[b])
            ratio = {j: square[i][j] * inverse for j in range(i + 1, width)}
            for j in range(i + 1, width):
                for m in range(i + 1, width):
                    square[m][j] = square[m][j] - square[m][i] * ratio[j]
                for t in below:
                    columns[j][t] = columns[j][t] - columns[i][t] * ratio[j]
                rows[j] = rows[j] - ratio[j] * rows[i]
            rows[i] = rows[i] * inverse
        for t in below:
            tile = tiles[t]
            for i in range(width):
                column = columns[i][t]
                if t == b:
                    column = jnp.where(row > r + i, column, 0.0)
                tile = tile - column * rows[i]
            tiles[t] = tile
    return [tile * lax.rsqrt(pivot) for tile, pivot in zip(tiles, pivots)]


def step_kernel(
    scale, v_ref, pot_ref, out_ref,
    own, pot, work, halo, panel, pieces, part, zbuf, gram, coef, inverse, rest,
    lsem, hsend, hrecv, asend, arecv, zsend, zrecv, gsend, grecv, near, far, ready,
):
    depth, count, plane = out_ref.shape
    nz, norb = lax.axis_size("grid"), lax.axis_size("orb")
    ny = norb // (2 * NXC)
    z, o = lax.axis_index("grid"), lax.axis_index("orb")
    y, x, c = o // (2 * NXC), (o // 2) % NXC, o % 2

    def at(yy, xx, cc):
        return (yy * NXC + xx) * 2 + cc

    partner = at(y, x, 1 - c)
    right, left = at(y, (x + 1) % NXC, c), at(y, (x + NXC - 1) % NXC, c)
    y_up, y_down = at((y + 1) % ny, x, c), at((y + ny - 1) % ny, x, c)
    z_up, z_down = (z + 1) % nz, (z + nz - 1) % nz
    order = order_of(depth)

    barrier = pltpu.get_barrier_semaphore()
    for peer in (z_up, z_down):
        pl.semaphore_signal(barrier, inc=1, device_id=(o, peer), device_id_type=MESH)
    for peer in (y_up, y_down, right, left, partner):
        pl.semaphore_signal(barrier, inc=1, device_id=(peer, z), device_id_type=MESH)
    load_v = pltpu.make_async_copy(v_ref, own, lsem.at[0])
    load_pot = pltpu.make_async_copy(pot_ref, pot, lsem.at[1])
    load_v.start()
    load_pot.start()
    pl.semaphore_wait(barrier, 7)

    arrived = {}
    for i in range(depth):
        for side, p, peer in ((0, depth - 1 - i, z_up), (1, i, z_down)):
            copy = pltpu.make_async_remote_copy(
                src_ref=v_ref.at[p],
                dst_ref=halo.at[side, p],
                send_sem=hsend.at[side, p],
                recv_sem=hrecv.at[side, p],
                device_id=(o, peer),
                device_id_type=MESH,
            )
            copy.start()
            arrived[side, p] = copy

    load_v.wait()
    load_pot.wait()

    def flat(p, carry):
        v = own[p]
        rest[p] = in_plane(v, (pot[pl.ds(p, 1), :] - 1.5 * COEFFS[0]) * v)
        return carry

    lax.fori_loop(0, depth, flat, 0)

    def slab(xx, cc):
        return (xx % NXC) * 2 + cc

    mine = slab(x, c)

    def copy_of(kind, s, p, peer):
        rows = pl.ds(pl.multiple_of(s * count, count), count)
        return pltpu.make_async_remote_copy(
            src_ref=panel.at[p, rows, :],
            dst_ref=panel.at[p, rows, :],
            send_sem=asend.at[kind, p],
            recv_sem=arecv.at[s, p],
            device_id=(peer, z),
            device_id_type=MESH,
        )

    goes_up = y <= ny // 2 - 1
    goes_down = (y == 0) | (y >= ny // 2 + 2)

    seen = set()
    for p in order:
        need = [(0, q) for q in range(p, depth)] + [(1, q) for q in range(0, p + 1)]
        for key in need:
            if key not in seen:
                seen.add(key)
                arrived[key].wait_recv()
        total = rest[p]
        for k in range(1, RIM + 1):
            after = own[p + k] if p + k < depth else halo[1, p + k - depth]
            before = own[p - k] if p - k >= 0 else halo[0, p - k + depth]
            total += (-0.5 * COEFFS[k]) * (after + before)
        work[p] = total

        @pl.when(y == 0)
        def _():
            panel[p, pl.ds(pl.multiple_of(mine * count, count), count), :] = total
            copy_of(0, mine, p, y_up).start()
            copy_of(1, mine, p, y_down).start()
            copy_of(2, mine, p, right).start()
            copy_of(3, mine, p, left).start()
            copy_of(5, mine, p, partner).start()

    for d in (2, nz - 2):
        pl.semaphore_signal(near, inc=1, device_id=(o, (z + d) % nz), device_id_type=MESH)

    lag_near, lag_far = LAGS
    for t in range(depth + lag_far):
        if t < depth:
            p = order[t]

            @pl.when(y != 0)
            def _():
                copy_of(0, mine, p, y_up).wait_recv()

                @pl.when(goes_up)
                def _():
                    copy_of(0, mine, p, y_up).start()

                @pl.when(goes_down)
                def _():
                    copy_of(1, mine, p, y_down).start()

                copy_of(2, mine, p, right).start()
                copy_of(3, mine, p, left).start()
                copy_of(5, mine, p, partner).start()
                if t == 0:
                    pl.semaphore_signal(ready, inc=1, device_id=(at(0, x, c), z), device_id_type=MESH)

        i = t - lag_near
        if 0 <= i < depth:
            p = order[i]
            from_left, from_right = slab(x + NXC - 1, c), slab(x + 1, c)
            copy_of(2, from_left, p, right).wait_recv()
            if i % 2 == 0:
                copy_of(4, from_left, p, right).start()
            copy_of(6, from_left, p, partner).start()
            copy_of(3, from_right, p, left).wait_recv()
            if i % 2 == 1:
                copy_of(4, from_right, p, left).start()
            copy_of(7, from_right, p, partner).start()
        i = t - lag_far
        if 0 <= i < depth:
            p = order[i]
            opposite = slab(x + 2, c)
            copy_of(4, opposite, p, right).wait_recv()
            copy_of(8, opposite, p, partner).start()

    pl.semaphore_wait(near, 2)
    for d in (4, nz - 4):
        pl.semaphore_signal(far, inc=1, device_id=(o, (z + d) % nz), device_id_type=MESH)

    part[...] = jnp.zeros_like(part)
    for p in order:
        for xx in range(NXC):
            copy_of(5, slab(xx, 1 - c), p, partner).wait_recv()
        high, low = split(panel[p])
        both = jnp.concatenate([high, low], axis=0)
        pieces[p] = both

        @pl.when(y == 0)
        def _():
            product = nt(both, both)
            part[...] += product[:ROWS] + product[ROWS:]

        @pl.when(y != 0)
        def _():
            own_high, own_low = split(work[p])
            product = nt(jnp.concatenate([own_high, own_low], axis=0), both)
            part[0:count] += product[:count] + product[count:]

    pl.semaphore_wait(far, 2)

    half_rows = ROWS // 2

    def z_copy(origin, to, slot, rows):
        return pltpu.make_async_remote_copy(
            src_ref=zbuf.at[origin, pl.ds(0, rows), :],
            dst_ref=zbuf.at[origin, pl.ds(0, rows), :],
            send_sem=zsend.at[slot],
            recv_sem=zrecv.at[origin],
            device_id=(o, to),
            device_id_type=MESH,
        )

    def z_send(rows):
        for i in range(nz // 2, 0, -1):
            for d in sorted({i, nz - i}):
                z_copy(z, (z + d) % nz, d, rows).start()

    def z_take(rows):
        def take(d, carry):
            z_copy((z + d) % nz, z, 0, rows).wait_recv()
            return carry

        lax.fori_loop(1, nz, take, 0)
        total = zbuf[0, 0:rows]
        for i in range(1, nz):
            total += zbuf[i, 0:rows]
        return total

    def z_done(rows):
        def done(d, carry):
            z_copy(z, (z + d) % nz, d, rows).wait_send()
            return carry

        lax.fori_loop(1, nz, done, 0)

    def g_copy(d):
        return pltpu.make_async_remote_copy(
            src_ref=gram,
            dst_ref=gram,
            send_sem=gsend.at[d],
            recv_sem=grecv,
            device_id=(at((y + d) % ny, x, c), z),
            device_id_type=MESH,
        )

    @pl.when(y == 0)
    def _():
        both = part[...]
        both = (both + pltpu.roll(both, ROWS, 1)) * scale
        lane = lax.broadcasted_iota(jnp.int32, (half_rows, 2 * ROWS), 1)
        zbuf[z] = jnp.where(lane < ROWS, both[:half_rows], both[half_rows:])
        z_send(half_rows)
        pl.semaphore_wait(ready, ny - 1)
        gram[...] = z_take(half_rows)
        for i in range(ny // 2, 0, -1):
            for d in sorted({i, ny - i}):
                g_copy(d).start()

    @pl.when(y != 0)
    def _():
        both = part[0:count]
        zbuf[z, 0:count] = (both + pltpu.roll(both, ROWS, 1)) * scale
        z_send(count)
        g_copy(1).wait_recv()

    tiles = eliminate(gram[...])
    for t, tile in enumerate(tiles):
        inverse[pl.ds(t * 8, 8), :] = tile
    lower_inverse = inverse[:, :ROWS]
    high = lax.Precision.HIGHEST
    solver = lax.dot_general(
        lower_inverse, lower_inverse, (((0,), (0,)), ((), ())), precision=high, preferred_element_type=F32
    )

    @pl.when(y == 0)
    def _():
        coef[...] = inverse[pl.ds(pl.multiple_of(mine * count, count), count), :]

    @pl.when(y != 0)
    def _():
        sums = z_take(count)[:, :ROWS]
        coef[:, :ROWS] = -jnp.dot(sums, solver, precision=high, preferred_element_type=F32)

    f_high, f_low = split(coef[:, :ROWS])
    factor = jnp.concatenate(
        [jnp.concatenate([f_high, f_high], axis=1), jnp.concatenate([f_low, f_low], axis=1)], axis=0
    )
    keep = jnp.where(y == 0, 0.0, 1.0)
    for p in range(depth):
        product = jnp.dot(factor, pieces[p], preferred_element_type=F32)
        out_ref[p] = keep * work[p] + (product[:count] + product[count:])

    for copy in arrived.values():
        copy.wait_send()
    for p in range(depth):

        @pl.when(goes_up)
        def _():
            copy_of(0, mine, p, y_up).wait_send()

        @pl.when(goes_down)
        def _():
            copy_of(1, mine, p, y_down).wait_send()

        for kind in range(2, 9):
            copy_of(kind, mine, p, partner).wait_send()

    @pl.when(y == 0)
    def _():
        z_done(half_rows)
        for d in range(1, ny):
            g_copy(d).wait_send()

    @pl.when(y != 0)
    def _():
        z_done(count)


def per_device(wavefunctions, potential):
    count, depth, plane = wavefunctions.shape
    nz, ny = lax.axis_size("grid"), lax.axis_size("orb") // (2 * NXC)
    scale = 1.0 / (depth * plane * nz)
    dma, plain = pltpu.SemaphoreType.DMA, pltpu.SemaphoreType.REGULAR
    out = pl.pallas_call(
        functools.partial(step_kernel, scale),
        out_shape=jax.ShapeDtypeStruct((depth, count, plane), F32),
        in_specs=[pl.BlockSpec(memory_space=pl.ANY)] * 2,
        out_specs=pl.BlockSpec(memory_space=pltpu.VMEM),
        scratch_shapes=[
            pltpu.VMEM((depth, count, plane), F32),
            pltpu.VMEM((depth, plane), F32),
            pltpu.VMEM((depth, count, plane), F32),
            pltpu.VMEM((2, depth, count, plane), F32),
            pltpu.VMEM((depth, ROWS, plane), F32),
            pltpu.VMEM((depth, 2 * ROWS, plane), BF16),
            pltpu.VMEM((ROWS, 2 * ROWS), F32),
            pltpu.VMEM((nz, ROWS // 2, 2 * ROWS), F32),
            pltpu.VMEM((ROWS // 2, 2 * ROWS), F32),
            pltpu.VMEM((count, 2 * ROWS), F32),
            pltpu.VMEM((ROWS, 2 * ROWS), F32),
            pltpu.VMEM((depth, count, plane), F32),
            dma((2,)),
            dma((2, depth)),
            dma((2, depth)),
            dma((9, depth)),
            dma((2 * NXC, depth)),
            dma((nz,)),
            dma((nz,)),
            dma((ny,)),
            dma,
            plain,
            plain,
            plain,
        ],
        compiler_params=pltpu.CompilerParams(collective_id=0, has_side_effects=True),
        name="step",
    )(jnp.transpose(wavefunctions, (1, 0, 2)), potential)
    return jnp.transpose(out, (1, 0, 2))


def solution(mesh):
    return jax.shard_map(
        per_device,
        mesh=mesh,
        in_specs=(P("orb", "grid", None), P("grid", None)),
        out_specs=P("orb", "grid", None),
        check_vma=False,
    )
```

time: 76.3 us -> 60.7 us (0.80)
  the two profiles are of different devices: /device:TPU:32 before, /device:TPU:8 now
where the time goes in v2:
time: 60.7 us; the launch traced here: 60.5 us
  Pallas kernels  58.9 us (97%)
  local copies, waits for them, and re-layouts  1.62 us (3%)
    pallas_call x1, Pallas kernels, per_device(): pl.pallas_call(functools.partial(step_kernel, scale), out_shape=jax.Shape...  58.9 us
    unnamed x1, local copies, waits for them, and re-layouts  1.62 us

profile of v2, /device:TPU:8, one launch (start us, length us, event | category | flops | bytes accessed | tf_op | source)
XLA Modules:
  0.0 60.5 jit_solution(14748035323240335242)
XLA Ops:
  0.0 58.9 %step.1 = f32[6,8,1024]{2,1,0:T(8,128)} custom-call(f32[6,8,1024]{2,1,0:T(8,128)} %bitcast.3, f32[6,1024]{1,0:T(8,128)} %pot_ref.1), custom_call_target="tpu_custom_call" | custom-call | tf_op jit(solution)/shard_map/step/pallas_call | solution.py:396
  58.9 1.6 %copy.4 = f32[8,6,1024]{2,0,1:T(8,128)} copy(f32[8,6,1024]{2,0,1:T(8,128)} %bitcast.2) | data formatting | bytes 393216

commit v3 on v2

--- a/solution.py
+++ b/solution.py
@@ -24,7 +24,7 @@
 )
 RIM = 6
 MESH = pl.DeviceIdType.MESH
-LAGS = (3, 6)
+BLOCK = 128
 F32 = jnp.float32
 BF16 = jnp.bfloat16
 
@@ -51,10 +51,6 @@
         part += jnp.where(column >= k, pltpu.roll(v, k, 1), 0.0)
         total += (-0.5 * COEFFS[k]) * part
     return total
-
-
-def order_of(depth):
-    return sorted(range(depth), key=lambda p: (max(depth - p, p + 1), p))
 
 
 def eliminate(packed):
@@ -121,7 +117,10 @@
     right, left = at(y, (x + 1) % NXC, c), at(y, (x + NXC - 1) % NXC, c)
     y_up, y_down = at((y + 1) % ny, x, c), at((y + ny - 1) % ny, x, c)
     z_up, z_down = (z + 1) % nz, (z + nz - 1) % nz
-    order = order_of(depth)
+    blocks = plane // BLOCK
+
+    def lanes(b):
+        return pl.ds(b * BLOCK, BLOCK)
 
     barrier = pltpu.get_barrier_semaphore()
     for peer in (z_up, z_down):
@@ -135,18 +134,18 @@
     pl.semaphore_wait(barrier, 7)
 
     arrived = {}
-    for i in range(depth):
-        for side, p, peer in ((0, depth - 1 - i, z_up), (1, i, z_down)):
+    for b in range(blocks):
+        for side, peer in ((0, z_up), (1, z_down)):
             copy = pltpu.make_async_remote_copy(
-                src_ref=v_ref.at[p],
-                dst_ref=halo.at[side, p],
-                send_sem=hsend.at[side, p],
-                recv_sem=hrecv.at[side, p],
+                src_ref=v_ref.at[:, :, lanes(b)],
+                dst_ref=halo.at[side, :, :, lanes(b)],
+                send_sem=hsend.at[side, b],
+                recv_sem=hrecv.at[side, b],
                 device_id=(o, peer),
                 device_id_type=MESH,
             )
             copy.start()
-            arrived[side, p] = copy
+            arrived[side, b] = copy
 
     load_v.wait()
     load_pot.wait()
@@ -163,13 +162,13 @@
 
     mine = slab(x, c)
 
-    def copy_of(kind, s, p, peer):
-        rows = pl.ds(pl.multiple_of(s * count, count), count)
+    def copy_of(kind, s, b, peer):
+        piece = panel.at[:, pl.ds(pl.multiple_of(s * count, count), count), lanes(b)]
         return pltpu.make_async_remote_copy(
-            src_ref=panel.at[p, rows, :],
-            dst_ref=panel.at[p, rows, :],
-            send_sem=asend.at[kind, p],
-            recv_sem=arecv.at[s, p],
+            src_ref=piece,
+            dst_ref=piece,
+            send_sem=asend.at[kind, b],
+            recv_sem=arecv.at[s, b],
             device_id=(peer, z),
             device_id_type=MESH,
         )
@@ -177,100 +176,119 @@
     goes_up = y <= ny // 2 - 1
     goes_down = (y == 0) | (y >= ny // 2 + 2)
 
-    seen = set()
-    for p in order:
-        need = [(0, q) for q in range(p, depth)] + [(1, q) for q in range(0, p + 1)]
-        for key in need:
-            if key not in seen:
-                seen.add(key)
-                arrived[key].wait_recv()
-        total = rest[p]
-        for k in range(1, RIM + 1):
-            after = own[p + k] if p + k < depth else halo[1, p + k - depth]
-            before = own[p - k] if p - k >= 0 else halo[0, p - k + depth]
-            total += (-0.5 * COEFFS[k]) * (after + before)
-        work[p] = total
+    for b in range(blocks):
+        for side in range(2):
+            arrived[side, b].wait_recv()
+        line = [halo[0, p, :, lanes(b)] for p in range(depth)]
+        line += [own[p, :, lanes(b)] for p in range(depth)]
+        line += [halo[1, p, :, lanes(b)] for p in range(depth)]
+        for p in range(depth):
+            total = rest[p, :, lanes(b)]
+            for k in range(1, RIM + 1):
+                total += (-0.5 * COEFFS[k]) * (line[depth + p + k] + line[depth + p - k])
+            work[p, :, lanes(b)] = total
 
         @pl.when(y == 0)
         def _():
-            panel[p, pl.ds(pl.multiple_of(mine * count, count), count), :] = total
-            copy_of(0, mine, p, y_up).start()
-            copy_of(1, mine, p, y_down).start()
-            copy_of(2, mine, p, right).start()
-            copy_of(3, mine, p, left).start()
-            copy_of(5, mine, p, partner).start()
+            for p in range(depth):
+                panel[p, pl.ds(pl.multiple_of(mine * count, count), count), lanes(b)] = work[p, :, lanes(b)]
+            copy_of(2, mine, b, right).start()
+            copy_of(3, mine, b, left).start()
+            copy_of(0, mine, b, y_up).start()
+            copy_of(1, mine, b, y_down).start()
+            copy_of(5, mine, b, partner).start()
 
     for d in (2, nz - 2):
         pl.semaphore_signal(near, inc=1, device_id=(o, (z + d) % nz), device_id_type=MESH)
 
-    lag_near, lag_far = LAGS
-    for t in range(depth + lag_far):
-        if t < depth:
-            p = order[t]
+    part[...] = jnp.zeros_like(part)
+
+    def inner_products(pair):
+        for b in (pair, pair + 1):
+            for xx in range(NXC):
+                copy_of(5, slab(xx, 1 - c), b, partner).wait_recv()
+        two = pl.ds(pair * BLOCK, 2 * BLOCK)
+        for p in range(depth):
+            high, low = split(panel[p, :, two])
+            pieces[p, :, two] = jnp.concatenate([high, low], axis=0)
+
+        @pl.when(y == 0)
+        def _():
+            total = jnp.zeros((2 * ROWS, 2 * ROWS), F32)
+            for p in range(depth):
+                both = pieces[p, :, two]
+                total += nt(both, both)
+            part[...] += total[:ROWS] + total[ROWS:]
+
+        @pl.when(y != 0)
+        def _():
+            total = jnp.zeros((2 * count, 2 * ROWS), F32)
+            for p in range(depth):
+                own_high, own_low = split(work[p, :, two])
+                total += nt(jnp.concatenate([own_high, own_low], axis=0), pieces[p, :, two])
+            part[0:count] += total[:count] + total[count:]
+
+    at_end = (x == 0) | (x == NXC - 1)
+    inside = (x > 0) & (x < NXC - 1)
+    relays = [at_end if b < blocks // 2 else inside for b in range(blocks)]
+
+    events = []
+    for i in range(blocks):
+        events.append((0.55 * i, 0, i))
+        events.append((2.6 + 0.8 * i, 1, i))
+        events.append((5.0 + 0.8 * i, 2, i))
+    from_left, from_right, opposite = slab(x + NXC - 1, c), slab(x + 1, c), slab(x + 2, c)
+    for _, what, chunk in sorted(events):
+        if what == 0:
 
             @pl.when(y != 0)
             def _():
-                copy_of(0, mine, p, y_up).wait_recv()
+                copy_of(0, mine, chunk, y_up).wait_recv()
 
                 @pl.when(goes_up)
                 def _():
-                    copy_of(0, mine, p, y_up).start()
+                    copy_of(0, mine, chunk, y_up).start()
 
                 @pl.when(goes_down)
                 def _():
-                    copy_of(1, mine, p, y_down).start()
-
-                copy_of(2, mine, p, right).start()
-                copy_of(3, mine, p, left).start()
-                copy_of(5, mine, p, partner).start()
-                if t == 0:
-                    pl.semaphore_signal(ready, inc=1, device_id=(at(0, x, c), z), device_id_type=MESH)
-
-        i = t - lag_near
-        if 0 <= i < depth:
-            p = order[i]
-            from_left, from_right = slab(x + NXC - 1, c), slab(x + 1, c)
-            copy_of(2, from_left, p, right).wait_recv()
-            if i % 2 == 0:
-                copy_of(4, from_left, p, right).start()
-            copy_of(6, from_left, p, partner).start()
-            copy_of(3, from_right, p, left).wait_recv()
-            if i % 2 == 1:
-                copy_of(4, from_right, p, left).start()
-            copy_of(7, from_right, p, partner).start()
-        i = t - lag_far
-        if 0 <= i < depth:
-            p = order[i]
-            opposite = slab(x + 2, c)
-            copy_of(4, opposite, p, right).wait_recv()
-            copy_of(8, opposite, p, partner).start()
+                    copy_of(1, mine, chunk, y_down).start()
+
+                copy_of(2, mine, chunk, right).start()
+                copy_of(3, mine, chunk, left).start()
+                copy_of(5, mine, chunk, partner).start()
+                if chunk == 0:
+                    for cc in range(2):
+                        pl.semaphore_signal(ready, inc=1, device_id=(at(0, x, cc), z), device_id_type=MESH)
+
+        elif what == 1:
+            copy_of(2, from_left, chunk, right).wait_recv()
+
+            @pl.when(relays[chunk])
+            def _():
+                copy_of(4, from_left, chunk, right).start()
+
+            copy_of(6, from_left, chunk, partner).start()
+            copy_of(3, from_right, chunk, left).wait_recv()
+
+            @pl.when(relays[chunk])
+            def _():
+                copy_of(9, from_right, chunk, left).start()
+
+            copy_of(7, from_right, chunk, partner).start()
+        else:
+            copy_of(4, opposite, chunk, right).wait_recv()
+            copy_of(8, opposite, chunk, partner).start()
 
     pl.semaphore_wait(near, 2)
     for d in (4, nz - 4):
         pl.semaphore_signal(far, inc=1, device_id=(o, (z + d) % nz), device_id_type=MESH)
 
-    part[...] = jnp.zeros_like(part)
-    for p in order:
-        for xx in range(NXC):
-            copy_of(5, slab(xx, 1 - c), p, partner).wait_recv()
-        high, low = split(panel[p])
-        both = jnp.concatenate([high, low], axis=0)
-        pieces[p] = both
-
-        @pl.when(y == 0)
-        def _():
-            product = nt(both, both)
-            part[...] += product[:ROWS] + product[ROWS:]
-
-        @pl.when(y != 0)
-        def _():
-            own_high, own_low = split(work[p])
-            product = nt(jnp.concatenate([own_high, own_low], axis=0), both)
-            part[0:count] += product[:count] + product[count:]
+    for pair in range(0, blocks, 2):
+        inner_products(pair)
 
     pl.semaphore_wait(far, 2)
 
-    half_rows = ROWS // 2
+    half_rows, quarter = ROWS // 2, ROWS // 4
 
     def z_copy(origin, to, slot, rows):
         return pltpu.make_async_remote_copy(
@@ -305,35 +323,42 @@
 
         lax.fori_loop(1, nz, done, 0)
 
-    def g_copy(d):
+    def g_copy(core, d, cc):
+        piece = gram.at[pl.ds(pl.multiple_of(core * quarter, quarter), quarter), :]
         return pltpu.make_async_remote_copy(
-            src_ref=gram,
-            dst_ref=gram,
-            send_sem=gsend.at[d],
-            recv_sem=grecv,
-            device_id=(at((y + d) % ny, x, c), z),
+            src_ref=piece,
+            dst_ref=piece,
+            send_sem=gsend.at[2 * d + (1 if cc is c else 0)],
+            recv_sem=grecv.at[core],
+            device_id=(at((y + d) % ny, x, cc), z),
             device_id_type=MESH,
         )
+
+    g_peers = [(d, cc) for i in range(ny // 2, 0, -1) for d in sorted({i, ny - i}) for cc in (c, 1 - c)]
+    g_peers.append((0, 1 - c))
 
     @pl.when(y == 0)
     def _():
         both = part[...]
         both = (both + pltpu.roll(both, ROWS, 1)) * scale
         lane = lax.broadcasted_iota(jnp.int32, (half_rows, 2 * ROWS), 1)
-        zbuf[z] = jnp.where(lane < ROWS, both[:half_rows], both[half_rows:])
-        z_send(half_rows)
-        pl.semaphore_wait(ready, ny - 1)
-        gram[...] = z_take(half_rows)
-        for i in range(ny // 2, 0, -1):
-            for d in sorted({i, ny - i}):
-                g_copy(d).start()
+        part[0:half_rows] = jnp.where(lane < ROWS, both[:half_rows], both[half_rows:])
+        zbuf[z] = part[pl.ds(pl.multiple_of(c * quarter, quarter), quarter), :]
+        z_send(quarter)
+        pl.semaphore_wait(ready, 2 * (ny - 1))
+        total = z_take(quarter)
+        gram[pl.ds(pl.multiple_of(c * quarter, quarter), quarter), :] = total
+        for d, cc in g_peers:
+            g_copy(c, d, cc).start()
+        g_copy(1 - c, 0, 1 - c).wait_recv()
 
     @pl.when(y != 0)
     def _():
         both = part[0:count]
         zbuf[z, 0:count] = (both + pltpu.roll(both, ROWS, 1)) * scale
         z_send(count)
-        g_copy(1).wait_recv()
+        for cc in range(2):
+            g_copy(cc, 0, c).wait_recv()
 
     tiles = eliminate(gram[...])
     for t, tile in enumerate(tiles):
@@ -364,34 +389,45 @@
 
     for copy in arrived.values():
         copy.wait_send()
-    for p in range(depth):
+    for b in range(blocks):
 
         @pl.when(goes_up)
         def _():
-            copy_of(0, mine, p, y_up).wait_send()
+            copy_of(0, mine, b, y_up).wait_send()
 
         @pl.when(goes_down)
         def _():
-            copy_of(1, mine, p, y_down).wait_send()
-
-        for kind in range(2, 9):
-            copy_of(kind, mine, p, partner).wait_send()
+            copy_of(1, mine, b, y_down).wait_send()
+
+        for kind in (2, 3, 5, 6, 7, 8):
+            copy_of(kind, mine, b, partner).wait_send()
+
+        @pl.when(relays[b])
+        def _():
+            copy_of(4, mine, b, partner).wait_send()
+            copy_of(9, mine, b, partner).wait_send()
 
     @pl.when(y == 0)
     def _():
-        z_done(half_rows)
-        for d in range(1, ny):
-            g_copy(d).wait_send()
+        z_done(quarter)
+        for d, cc in g_peers:
+            g_copy(c, d, cc).wait_send()
 
     @pl.when(y != 0)
     def _():
         z_done(count)
+
+
+def store_kernel(value_ref, out_ref, sem):
+    copy = pltpu.make_async_copy(value_ref, out_ref, sem)
+    copy.start()
+    copy.wait()
 
 
 def per_device(wavefunctions, potential):
     count, depth, plane = wavefunctions.shape
     nz, ny = lax.axis_size("grid"), lax.axis_size("orb") // (2 * NXC)
-    scale = 1.0 / (depth * plane * nz)
+    scale, blocks = 1.0 / (depth * plane * nz), plane // BLOCK
     dma, plain = pltpu.SemaphoreType.DMA, pltpu.SemaphoreType.REGULAR
     out = pl.pallas_call(
         functools.partial(step_kernel, scale),
@@ -406,27 +442,39 @@
             pltpu.VMEM((depth, ROWS, plane), F32),
             pltpu.VMEM((depth, 2 * ROWS, plane), BF16),
             pltpu.VMEM((ROWS, 2 * ROWS), F32),
-            pltpu.VMEM((nz, ROWS // 2, 2 * ROWS), F32),
+            pltpu.VMEM((nz, ROWS // 4, 2 * ROWS), F32),
             pltpu.VMEM((ROWS // 2, 2 * ROWS), F32),
             pltpu.VMEM((count, 2 * ROWS), F32),
             pltpu.VMEM((ROWS, 2 * ROWS), F32),
             pltpu.VMEM((depth, count, plane), F32),
             dma((2,)),
-            dma((2, depth)),
-            dma((2, depth)),
-            dma((9, depth)),
-            dma((2 * NXC, depth)),
+            dma((2, blocks)),
+            dma((2, blocks)),
+            dma((10, blocks)),
+            dma((2 * NXC, blocks)),
             dma((nz,)),
             dma((nz,)),
-            dma((ny,)),
-            dma,
+            dma((2 * ny,)),
+            dma((2,)),
             plain,
             plain,
             plain,
         ],
-        compiler_params=pltpu.CompilerParams(collective_id=0, has_side_effects=True),
+        compiler_params=pltpu.CompilerParams(collective_id=0, has_side_effects=True, vmem_limit_bytes=8 << 20),
         name="step",
-    )(jnp.transpose(wavefunctions, (1, 0, 2)), potential)
+    )(
+        pltpu.with_memory_space_constraint(jnp.transpose(wavefunctions, (1, 0, 2)), pltpu.MemorySpace.HBM),
+        pltpu.with_memory_space_constraint(potential, pltpu.MemorySpace.HBM),
+    )
+    out = pl.pallas_call(
+        store_kernel,
+        out_shape=jax.ShapeDtypeStruct((depth, count, plane), F32),
+        in_specs=[pl.BlockSpec(memory_space=pl.ANY)],
+        out_specs=pl.BlockSpec(memory_space=pl.ANY),
+        scratch_shapes=[pltpu.SemaphoreType.DMA],
+        compiler_params=pltpu.CompilerParams(vmem_limit_bytes=1 << 20),
+        name="store",
+    )(out)
     return jnp.transpose(out, (1, 0, 2))
 
 

time: 60.7 us -> 58 us (0.956)
  the two profiles are of different devices: /device:TPU:8 before, /device:TPU:34 now
where the time goes in v3:
time: 58 us; the launch traced here: 57.9 us
  Pallas kernels  57.9 us (100%)
    pallas_call x1, Pallas kernels, per_device(): pl.pallas_call(functools.partial(step_kernel, scale), out_shape=jax.Shape...  57.2 us

profile of v3, /device:TPU:34, one launch (start us, length us, event | category | flops | bytes accessed | tf_op | source)
XLA Modules:
  0.0 57.9 jit_solution(3570324380073553721)
XLA Ops:
  0.0 57.2 %step.1.value_ref = f32[6,8,1024]{2,1,0:T(8,128)S(1)} custom-call(f32[6,8,1024]{2,1,0:T(8,128)} %bitcast.2, f32[6,1024]{1,0:T(8,128)} %pot_ref.1), custom_call_target="tpu_custom_call" | custom-call | tf_op jit(solution)/shard_map/step/pallas_call | solution.py:432
  57.2 0.7 %store.1 = f32[6,8,1024]{2,1,0:T(8,128)} custom-call(f32[6,8,1024]{2,1,0:T(8,128)S(1)} %step.1.value_ref), custom_call_target="tpu_custom_call" | custom-call | tf_op jit(solution)/shard_map/store/pallas_call | solution.py:469

commit v4 on v3

--- a/solution.py
+++ b/solution.py
@@ -24,6 +24,7 @@
 )
 RIM = 6
 MESH = pl.DeviceIdType.MESH
+GREET = 6
 BLOCK = 128
 F32 = jnp.float32
 BF16 = jnp.bfloat16
@@ -275,13 +276,13 @@
                 copy_of(9, from_right, chunk, left).start()
 
             copy_of(7, from_right, chunk, partner).start()
+            if chunk == GREET:
+                pl.semaphore_wait(near, 2)
+                for d in (4, nz - 4):
+                    pl.semaphore_signal(far, inc=1, device_id=(o, (z + d) % nz), device_id_type=MESH)
         else:
             copy_of(4, opposite, chunk, right).wait_recv()
             copy_of(8, opposite, chunk, partner).start()
-
-    pl.semaphore_wait(near, 2)
-    for d in (4, nz - 4):
-        pl.semaphore_signal(far, inc=1, device_id=(o, (z + d) % nz), device_id_type=MESH)
 
     for pair in range(0, blocks, 2):
         inner_products(pair)
@@ -337,6 +338,27 @@
     g_peers = [(d, cc) for i in range(ny // 2, 0, -1) for d in sorted({i, ny - i}) for cc in (c, 1 - c)]
     g_peers.append((0, 1 - c))
 
+    def all_left():
+        for copy in arrived.values():
+            copy.wait_send()
+        for b in range(blocks):
+
+            @pl.when(goes_up)
+            def _():
+                copy_of(0, mine, b, y_up).wait_send()
+
+            @pl.when(goes_down)
+            def _():
+                copy_of(1, mine, b, y_down).wait_send()
+
+            for kind in (2, 3, 5, 6, 7, 8):
+                copy_of(kind, mine, b, partner).wait_send()
+
+            @pl.when(relays[b])
+            def _():
+                copy_of(4, mine, b, partner).wait_send()
+                copy_of(9, mine, b, partner).wait_send()
+
     @pl.when(y == 0)
     def _():
         both = part[...]
@@ -345,6 +367,7 @@
         part[0:half_rows] = jnp.where(lane < ROWS, both[:half_rows], both[half_rows:])
         zbuf[z] = part[pl.ds(pl.multiple_of(c * quarter, quarter), quarter), :]
         z_send(quarter)
+        all_left()
         pl.semaphore_wait(ready, 2 * (ny - 1))
         total = z_take(quarter)
         gram[pl.ds(pl.multiple_of(c * quarter, quarter), quarter), :] = total
@@ -357,6 +380,7 @@
         both = part[0:count]
         zbuf[z, 0:count] = (both + pltpu.roll(both, ROWS, 1)) * scale
         z_send(count)
+        all_left()
         for cc in range(2):
             g_copy(cc, 0, c).wait_recv()
 
@@ -386,26 +410,6 @@
     for p in range(depth):
         product = jnp.dot(factor, pieces[p], preferred_element_type=F32)
         out_ref[p] = keep * work[p] + (product[:count] + product[count:])
-
-    for copy in arrived.values():
-        copy.wait_send()
-    for b in range(blocks):
-
-        @pl.when(goes_up)
-        def _():
-            copy_of(0, mine, b, y_up).wait_send()
-
-        @pl.when(goes_down)
-        def _():
-            copy_of(1, mine, b, y_down).wait_send()
-
-        for kind in (2, 3, 5, 6, 7, 8):
-            copy_of(kind, mine, b, partner).wait_send()
-
-        @pl.when(relays[b])
-        def _():
-            copy_of(4, mine, b, partner).wait_send()
-            copy_of(9, mine, b, partner).wait_send()
 
     @pl.when(y == 0)
     def _():

time: 58 us -> 56.1 us (0.967)
  the two profiles are of different devices: /device:TPU:34 before, /device:TPU:32 now
where the time goes in v4:
time: 56.1 us; the launch traced here: 56 us
  Pallas kernels  56 us (100%)
    pallas_call x1, Pallas kernels, per_device(): pl.pallas_call(functools.partial(step_kernel, scale), out_shape=jax.Shape...  55.3 us

profile of v4, /device:TPU:32, one launch (start us, length us, event | category | flops | bytes accessed | tf_op | source)
XLA Modules:
  0.0 56.0 jit_solution(11961192469963011224)
XLA Ops:
  0.0 55.3 %step.1.value_ref = f32[6,8,1024]{2,1,0:T(8,128)S(1)} custom-call(f32[6,8,1024]{2,1,0:T(8,128)} %bitcast.2, f32[6,1024]{1,0:T(8,128)} %pot_ref.1), custom_call_target="tpu_custom_call" | custom-call | tf_op jit(solution)/shard_map/step/pallas_call | solution.py:436
  55.3 0.7 %store.1 = f32[6,8,1024]{2,1,0:T(8,128)} custom-call(f32[6,8,1024]{2,1,0:T(8,128)S(1)} %step.1.value_ref), custom_call_target="tpu_custom_call" | custom-call | tf_op jit(solution)/shard_map/store/pallas_call | solution.py:473

commit v5 on v4

--- a/solution.py
+++ b/solution.py
@@ -24,8 +24,8 @@
 )
 RIM = 6
 MESH = pl.DeviceIdType.MESH
-GREET = 6
-BLOCK = 128
+GREET = 2
+BLOCK = 256
 F32 = jnp.float32
 BF16 = jnp.bfloat16
 
@@ -68,7 +68,7 @@
     def spread(tile, r):
         return jnp.broadcast_to(tile[r : r + 1, :], tile.shape)
 
-    width = 4
+    width = 8
     for k in range(0, ROWS, width):
         b, r = k // 8, k % 8
         below = range(b, ROWS // 8)
@@ -235,9 +235,9 @@
 
     events = []
     for i in range(blocks):
-        events.append((0.55 * i, 0, i))
-        events.append((2.6 + 0.8 * i, 1, i))
-        events.append((5.0 + 0.8 * i, 2, i))
+        events.append((1.1 * i, 0, i))
+        events.append((3.1 + 1.6 * i, 1, i))
+        events.append((6.0 + 1.6 * i, 2, i))
     from_left, from_right, opposite = slab(x + NXC - 1, c), slab(x + 1, c), slab(x + 2, c)
     for _, what, chunk in sorted(events):
         if what == 0:

time: 56.1 us -> 55.9 us (level)
  no operation moved by 1% of the time
where the time goes in v5:
time: 55.9 us; the launch traced here: 55.5 us
  Pallas kernels  55.5 us (99%)
    pallas_call x1, Pallas kernels, per_device(): pl.pallas_call(functools.partial(step_kernel, scale), out_shape=jax.Shape...  54.8 us

profile of v5, /device:TPU:32, one launch (start us, length us, event | category | flops | bytes accessed | tf_op | source)
XLA Modules:
  0.0 55.5 jit_solution(3551655230288654654)
XLA Ops:
  0.0 54.8 %step.1.value_ref = f32[6,8,1024]{2,1,0:T(8,128)S(1)} custom-call(f32[6,8,1024]{2,1,0:T(8,128)} %bitcast.2, f32[6,1024]{1,0:T(8,128)} %pot_ref.1), custom_call_target="tpu_custom_call" | custom-call | tf_op jit(solution)/shard_map/step/pallas_call | solution.py:436
  54.8 0.7 %store.1 = f32[6,8,1024]{2,1,0:T(8,128)} custom-call(f32[6,8,1024]{2,1,0:T(8,128)S(1)} %step.1.value_ref), custom_call_target="tpu_custom_call" | custom-call | tf_op jit(solution)/shard_map/store/pallas_call | solution.py:473

commit v6 on v5

--- a/solution.py
+++ b/solution.py
@@ -193,10 +193,10 @@
         def _():
             for p in range(depth):
                 panel[p, pl.ds(pl.multiple_of(mine * count, count), count), lanes(b)] = work[p, :, lanes(b)]
+            copy_of(0, mine, b, y_up).start()
+            copy_of(1, mine, b, y_down).start()
             copy_of(2, mine, b, right).start()
             copy_of(3, mine, b, left).start()
-            copy_of(0, mine, b, y_up).start()
-            copy_of(1, mine, b, y_down).start()
             copy_of(5, mine, b, partner).start()
 
     for d in (2, nz - 2):

time: 55.9 us -> 55.9 us (level)
  no operation moved by 1% of the time
where the time goes in v6:
time: 55.9 us; the launch traced here: 55.5 us
  Pallas kernels  55.5 us (99%)
    pallas_call x1, Pallas kernels, per_device(): pl.pallas_call(functools.partial(step_kernel, scale), out_shape=jax.Shape...  54.8 us

profile of v6, /device:TPU:32, one launch (start us, length us, event | category | flops | bytes accessed | tf_op | source)
XLA Modules:
  0.0 55.5 jit_solution(8977376286930871417)
XLA Ops:
  0.0 54.8 %step.1.value_ref = f32[6,8,1024]{2,1,0:T(8,128)S(1)} custom-call(f32[6,8,1024]{2,1,0:T(8,128)} %bitcast.2, f32[6,1024]{1,0:T(8,128)} %pot_ref.1), custom_call_target="tpu_custom_call" | custom-call | tf_op jit(solution)/shard_map/step/pallas_call | solution.py:436
  54.8 0.7 %store.1 = f32[6,8,1024]{2,1,0:T(8,128)} custom-call(f32[6,8,1024]{2,1,0:T(8,128)S(1)} %step.1.value_ref), custom_call_target="tpu_custom_call" | custom-call | tf_op jit(solution)/shard_map/store/pallas_call | solution.py:473
